TPU v7x, 128 devices: a whole 4x4x4 slice. The times are simulated.
128 devices in a mesh: view: 8 (over y_hi, x), gz: 16 (over z, y_lo, core).
Axes of the slice: x: 4, y: 4 (y_hi: 2, y_lo: 2; y = y_hi * 2 + y_lo), z: 4, core: 2. Of those that a mesh axis runs over, the one named last changes fastest.
Arguments:
- views_data: float32 [8, 256, 96, 1024], P('view', 'gz'), may hold values from 0.2 to 40
- estimate: float32 [256, 96, 1024], P('gz'), may hold values from 0.5 to 1.5
- kernels: float32 [8, 3, 31], P('view'), may hold values from 0.001 to 3
Outputs:
- deconvolved: float32 [256, 96, 1024], P('gz')
All inputs are finite; a program needn't handle non-finite values.
Results may differ from a plain program's by a relative error of at most 0.0001.
Values sent between devices are 32-bit elements; how exact they have to be, the bound alone decides.
No kernel may reach another device: no remote copies, remote signals or barrier semaphores. Data moves between devices by JAX's collectives and lax.ppermute only.
A program may use at most 128 MiB of HBM per device.

v0:
```python
import jax
import jax.numpy as jnp
from jax import lax
from jax.sharding import PartitionSpec as P

TAPS = 31
ITERS = 2
RADIUS = 15


def padded_2(value, sides, width):
    for axis, dim in sides:
        size, length = (lax.axis_size(axis), value.shape[dim])
        up = [(i, (i + 1) % size) for i in range(size - 1)]
        down = [(j, i) for i, j in up]
        last = lax.slice_in_dim(value, length - width, length, axis=dim)
        initial = lax.slice_in_dim(value, 0, width, axis=dim)
        before = lax.ppermute(last, axis, up)
        after = lax.ppermute(initial, axis, down)
        value = jnp.concatenate([before, value, after], axis=dim)
    return value


def toeplitz(tap_values, count):
    row_pos = jnp.arange(count)[:, None]
    col_pos = jnp.arange(count)[None, :]
    offsets = row_pos - col_pos + RADIUS
    matrix = jnp.zeros((count, count), jnp.float32)
    for offset in range(TAPS):
        matrix = matrix + jnp.where(offsets == offset, tap_values[offset], 0.0)
    return matrix


def tap_sum(padded, tap_values, flipped, depth):
    result = jnp.zeros((depth,) + padded.shape[1:], jnp.float32)
    for offset in range(TAPS):
        start = 2 * RADIUS - offset if flipped else offset
        result = result + tap_values[offset] * padded[start : start + depth]
    return result


def z_pass(volume, tap_values, flipped):
    padded = padded_2(volume, (("gz", 0),), RADIUS)
    return tap_sum(padded, tap_values, flipped, volume.shape[0])


def xy_pass(volume, mat_x, mat_y):
    passed = jnp.dot(volume, mat_x, precision=lax.Precision.HIGHEST)
    return jnp.einsum("zyx,yw->zwx", passed, mat_y, precision=lax.Precision.HIGHEST)


def per_device(views_data, estimate, kernels):
    tap_norm = kernels[0] / jnp.sum(kernels[0], axis=-1, keepdims=True)
    data_slab = views_data[0]
    mat_x = toeplitz(tap_norm[0], estimate.shape[2])
    mat_y = toeplitz(tap_norm[1], estimate.shape[1])
    views_count = lax.axis_size("view")
    for number in range(ITERS):
        blurred = z_pass(xy_pass(estimate, mat_x, mat_y), tap_norm[2], False)
        ratio = data_slab / blurred
        back = z_pass(xy_pass(ratio, mat_x.T, mat_y.T), tap_norm[2], True)
        logs = jnp.log(back)
        logsum = lax.psum(logs, "view")
        estimate = estimate * jnp.exp(logsum / views_count)
    return estimate


def solution(mesh):
    return jax.shard_map(
        per_device,
        mesh=mesh,
        in_specs=(P("view", "gz", None, None), P("gz", None, None), P("view", None, None)),
        out_specs=P("gz", None, None),
        check_vma=False,
    )
```

profile of v0, /device:TPU:1, one launch (start us, length us, event | category | flops | bytes accessed | tf_op | source)
XLA Modules:
  0.0 1528.6 jit_solution(3375969861306123260)
XLA Ops:
  11.0 45.9 %fusion.432 = f32[1024,16,96]{0,2,1:T(8,128)S(1)} fusion(f32[16,96,1024]{2,1,0:T(8,128)} %param.4, f32[]{:T(128)} %bitcast.65, f32[]{:T(128)} %bitcast.64, f32[]{:T(128)} %bitcast.63, f32[]{:T(128)} %bitcast.62, f32[]{:T(128)} %bitcast.61, f32[]{:T(128)} %bitcast.60, f32[]{:T(128)} %bitcast.59, f32[]{:T(128)} %bitcast.58, f32[]{:T(128)} %bitcast.57, ...), kind=kOutput, calls=%fused_computation.606 | convolution fusion | flops 19425918976 | bytes 12583036 | tf_op jit(solution)/shard_map/dot_general | solution.py:48
  56.9 26.1 %fusion.527 = f32[16,96,1024]{2,1,0:T(8,128)S(1)} fusion(f32[1024,16,96]{0,2,1:T(8,128)S(1)} %fusion.432, f32[]{:T(128)} %bitcast.31, f32[]{:T(128)} %bitcast.30, f32[]{:T(128)} %bitcast.29, f32[]{:T(128)} %bitcast.28, f32[]{:T(128)} %bitcast.27, f32[]{:T(128)} %bitcast.26, f32[]{:T(128)} %bitcast.25, f32[]{:T(128)} %bitcast.24, f32[]{:T(128)} %bitcast.23, ...), kind=kOutput, calls=%fused_computation.703 | convolution fusion | flops 1812805632 | bytes 12583036 | tf_op jit(solution)/shard_map/zyx,yw->zwx/dot_general | solution.py:49
  83.0 6.4 fusion.827
  89.4 4.6 collective-permute-start
  97.2 60.8 %collective-permute-done = f32[15,96,1024]{2,1,0:T(8,128)} collective-permute-done((f32[15,96,1024]{2,1,0:T(8,128)}, f32[15,96,1024]{2,1,0:T(8,128)}, u32[]{:S(2)}, u32[]{:S(2)}) %collective-permute-start) | collective-permute-done | bytes 5898272 | tf_op jit(solution)/shard_map/ppermute | solution.py:18
  158.0 65.2 %collective-permute-done.1 = f32[15,96,1024]{2,1,0:T(8,128)} collective-permute-done((f32[15,96,1024]{2,1,0:T(8,128)}, f32[15,96,1024]{2,1,0:T(8,128)}, u32[]{:S(2)}, u32[]{:S(2)}) %collective-permute-start.1) | collective-permute-done | bytes 5898272 | tf_op jit(solution)/shard_map/ppermute | solution.py:19
  223.1 153.6 %fusion.295 = f32[16,96,1024]{2,1,0:T(8,128)} fusion(f32[16,96,1024]{2,1,0:T(8,128)} %copy-done.1, f32[15,96,1024]{2,1,0:T(8,128)} %collective-permute-done.1, f32[15,96,1024]{2,1,0:T(8,128)} %collective-permute-done, f32[1,16,96,1024]{3,2,1,0:T(8,128)} %param.3, f32[]{:T(128)} %bitcast.98, f32[]{:T(128)} %bitcast.97, f32[]{:T(128)} %bitcast.96, ...), kind=kOutput, calls=%fused_computation.491 | convolution fusion | flops 19570622464 | bytes 30671096 | tf_op jit(solution)/shard_map/dot_general | solution.py:48
  376.7 27.5 %convolution_bitcast_fusion.2 = f32[16,96,1024]{2,1,0:T(8,128)S(1)} fusion(f32[16,96,1024]{2,1,0:T(8,128)} %fusion.295, f32[]{:T(128)} %bitcast.31, f32[]{:T(128)} %bitcast.30, f32[]{:T(128)} %bitcast.29, f32[]{:T(128)} %bitcast.28, f32[]{:T(128)} %bitcast.27, f32[]{:T(128)} %bitcast.26, f32[]{:T(128)} %bitcast.25, f32[]{:T(128)} %bitcast.24, ...), kind=kOutput, calls=%fused_computation.706 | convolution fusion | flops 1812805632 | bytes 12583036 | tf_op jit(solution)/shard_map/zyx,yw->zwx/dot_general | solution.py:49
  404.2 6.0 fusion.826
  415.9 121.8 %collective-permute-done.2 = f32[15,96,1024]{2,1,0:T(8,128)} collective-permute-done((f32[15,96,1024]{2,1,0:T(8,128)}, f32[15,96,1024]{2,1,0:T(8,128)}, u32[]{:S(2)}, u32[]{:S(2)}) %collective-permute-start.2) | collective-permute-done | bytes 5898272 | tf_op jit(solution)/shard_map/ppermute | solution.py:19
  537.7 64.1 %fusion.207 = f32[16,96,1024]{2,1,0:T(8,128)} fusion(f32[16,96,1024]{2,1,0:T(8,128)S(1)} %convolution_bitcast_fusion.2, f32[15,96,1024]{2,1,0:T(8,128)} %collective-permute-done.3, f32[15,96,1024]{2,1,0:T(8,128)} %collective-permute-done.2, f32[]{:T(128)} %bitcast.98, f32[]{:T(128)} %bitcast.97, f32[]{:T(128)} %bitcast.96, f32[]{:T(128)} %bitcast.95, ...), kind=kLoop, calls=%fused_computation.403 | loop fusion | flops 143130624 | bytes 24379516 | tf_op jit(solution)/shard_map/log | solution.py:62
  601.9 152.4 %all-reduce.3.cloned.1.call-done = f32[16,96,1024]{2,1,0:T(8,128)} async-done(((f32[16,96,1024]{2,1,0:T(8,128)}), f32[16,96,1024]{2,1,0:T(8,128)}) %all-reduce.3.cloned.1.call-update) | async-done | bytes 6291472 | tf_op jit(solution)/shard_map/psum | solution.py:63
  754.3 66.6 %fusion.429 = f32[16,96,1024]{2,1,0:T(8,128)S(1)} fusion(f32[]{:T(128)} %bitcast.65, f32[]{:T(128)} %bitcast.64, f32[]{:T(128)} %bitcast.63, f32[]{:T(128)} %bitcast.62, f32[]{:T(128)} %bitcast.61, f32[]{:T(128)} %bitcast.60, f32[]{:T(128)} %bitcast.59, f32[]{:T(128)} %bitcast.58, f32[]{:T(128)} %bitcast.57, f32[]{:T(128)} %bitcast.56, f32[]{:T(128)} %bitcast.55, ...), kind=kOutput, calls=%fused_computation.603 | convolution fusion | flops 19429064704 | bytes 18874492 | tf_op jit(solution)/shard_map/dot_general | solution.py:48
  820.9 25.7 %convolution_bitcast_fusion.1 = f32[16,96,1024]{2,1,0:T(8,128)S(1)} fusion(f32[16,96,1024]{2,1,0:T(8,128)S(1)} %fusion.429, f32[]{:T(128)} %bitcast.31, f32[]{:T(128)} %bitcast.30, f32[]{:T(128)} %bitcast.29, f32[]{:T(128)} %bitcast.28, f32[]{:T(128)} %bitcast.27, f32[]{:T(128)} %bitcast.26, f32[]{:T(128)} %bitcast.25, f32[]{:T(128)} %bitcast.24, ...), kind=kOutput, calls=%fused_computation.705 | convolution fusion | flops 1812805632 | bytes 12583036 | tf_op jit(solution)/shard_map/zyx,yw->zwx/dot_general | solution.py:49
  846.7 6.4 fusion.825
  859.8 60.0 %collective-permute-done.4 = f32[15,96,1024]{2,1,0:T(8,128)} collective-permute-done((f32[15,96,1024]{2,1,0:T(8,128)}, f32[15,96,1024]{2,1,0:T(8,128)}, u32[]{:S(2)}, u32[]{:S(2)}) %collective-permute-start.4) | collective-permute-done | bytes 5898272 | tf_op jit(solution)/shard_map/ppermute | solution.py:18
  919.8 65.8 %collective-permute-done.5 = f32[15,96,1024]{2,1,0:T(8,128)} collective-permute-done((f32[15,96,1024]{2,1,0:T(8,128)}, f32[15,96,1024]{2,1,0:T(8,128)}, u32[]{:S(2)}, u32[]{:S(2)}) %collective-permute-start.5) | collective-permute-done | bytes 5898272 | tf_op jit(solution)/shard_map/ppermute | solution.py:19
  985.6 153.0 %fusion.92 = f32[16,96,1024]{2,1,0:T(8,128)} fusion(f32[16,96,1024]{2,1,0:T(8,128)} %copy-done, f32[15,96,1024]{2,1,0:T(8,128)} %collective-permute-done.5, f32[15,96,1024]{2,1,0:T(8,128)} %collective-permute-done.4, f32[1,16,96,1024]{3,2,1,0:T(8,128)} %param.3, f32[]{:T(128)} %bitcast.98, f32[]{:T(128)} %bitcast.97, f32[]{:T(128)} %bitcast.96, ...), kind=kOutput, calls=%fused_computation.316 | convolution fusion | flops 19570622464 | bytes 30671096 | tf_op jit(solution)/shard_map/dot_general | solution.py:48
  1138.6 27.5 %convolution_bitcast_fusion = f32[16,96,1024]{2,1,0:T(8,128)S(1)} fusion(f32[16,96,1024]{2,1,0:T(8,128)} %fusion.92, f32[]{:T(128)} %bitcast.31, f32[]{:T(128)} %bitcast.30, f32[]{:T(128)} %bitcast.29, f32[]{:T(128)} %bitcast.28, f32[]{:T(128)} %bitcast.27, f32[]{:T(128)} %bitcast.26, f32[]{:T(128)} %bitcast.25, f32[]{:T(128)} %bitcast.24, f32[]{:T(128)} %bitcast.23, ...), kind=kOutput, calls=%fused_computation.704 | convolution fusion | flops 1812805632 | bytes 12583036 | tf_op jit(solution)/shard_map/zyx,yw->zwx/dot_general | solution.py:49
  1166.1 6.0 fusion.824
  1177.9 122.6 %collective-permute-done.6 = f32[15,96,1024]{2,1,0:T(8,128)} collective-permute-done((f32[15,96,1024]{2,1,0:T(8,128)}, f32[15,96,1024]{2,1,0:T(8,128)}, u32[]{:S(2)}, u32[]{:S(2)}) %collective-permute-start.6) | collective-permute-done | bytes 5898272 | tf_op jit(solution)/shard_map/ppermute | solution.py:19
  1300.5 64.0 %fusion.4 = f32[16,96,1024]{2,1,0:T(8,128)} fusion(f32[16,96,1024]{2,1,0:T(8,128)S(1)} %convolution_bitcast_fusion, f32[15,96,1024]{2,1,0:T(8,128)} %collective-permute-done.7, f32[15,96,1024]{2,1,0:T(8,128)} %collective-permute-done.6, f32[]{:T(128)} %bitcast.98, f32[]{:T(128)} %bitcast.97, f32[]{:T(128)} %bitcast.96, f32[]{:T(128)} %bitcast.95, ...), kind=kLoop, calls=%fused_computation.228 | loop fusion | flops 143130624 | bytes 24379516 | tf_op jit(solution)/shard_map/log | solution.py:62
  1364.5 146.9 %all-reduce.5.cloned.1.call-done = f32[16,96,1024]{2,1,0:T(8,128)} async-done(((f32[16,96,1024]{2,1,0:T(8,128)}), f32[16,96,1024]{2,1,0:T(8,128)}) %all-reduce.5.cloned.1.call-update) | async-done | bytes 6291472 | tf_op jit(solution)/shard_map/psum | solution.py:63
  1511.4 9.9 exponential_multiply_fusion
  (24 shorter events, 26.1 us)
Async XLA Ops:
  6.5 747.8 %all-reduce.3.cloned.1.call-start = ((), (), s32[]{:S(2)}) async-start(), calls=%async_computation | async-start | bytes 12582912 | tf_op jit(solution)/shard_map/psum | solution.py:63
  83.0 6.4 copy-start.1
  89.4 68.6 %collective-permute-start = (f32[15,96,1024]{2,1,0:T(8,128)}, f32[15,96,1024]{2,1,0:T(8,128)}, u32[]{:S(2)}, u32[]{:S(2)}) collective-permute-start(f32[15,96,1024]{2,1,0:T(8,128)} %get-tuple-element.11), channel_id=1, source_target_pairs={{0,1},{1,2},{2,3},{3,4},{4,5},{5,6},{6,7},{7,8},{8,9},{9,10},{10,1... | collective-permute-start | bytes 17694728 | tf_op jit(solution)/shard_map/ppermute | solution.py:18
  94.0 129.2 %collective-permute-start.1 = (f32[15,96,1024]{2,1,0:T(8,128)}, f32[15,96,1024]{2,1,0:T(8,128)}, u32[]{:S(2)}, u32[]{:S(2)}) collective-permute-start(f32[15,96,1024]{2,1,0:T(8,128)} %get-tuple-element.12), channel_id=1, source_target_pairs={{1,0},{2,1},{3,2},{4,3},{5,4},{6,5},{7,6},{8,7},{9,8},{10,9},{11,1... | collective-permute-start | bytes 17694728 | tf_op jit(solution)/shard_map/ppermute | solution.py:19
  410.2 127.5 %collective-permute-start.2 = (f32[15,96,1024]{2,1,0:T(8,128)}, f32[15,96,1024]{2,1,0:T(8,128)}, u32[]{:S(2)}, u32[]{:S(2)}) collective-permute-start(f32[15,96,1024]{2,1,0:T(8,128)} %get-tuple-element.9), channel_id=1, source_target_pairs={{1,0},{2,1},{3,2},{4,3},{5,4},{6,5},{7,6},{8,7},{9,8},{10,9},{11,1... | collective-permute-start | bytes 17694728 | tf_op jit(solution)/shard_map/ppermute | solution.py:19
  412.3 125.4 %collective-permute-start.3 = (f32[15,96,1024]{2,1,0:T(8,128)}, f32[15,96,1024]{2,1,0:T(8,128)}, u32[]{:S(2)}, u32[]{:S(2)}) collective-permute-start(f32[15,96,1024]{2,1,0:T(8,128)} %get-tuple-element.10), channel_id=1, source_target_pairs={{0,1},{1,2},{2,3},{3,4},{4,5},{5,6},{6,7},{7,8},{8,9},{9,10},{10,1... | collective-permute-start | bytes 17694728 | tf_op jit(solution)/shard_map/ppermute | solution.py:18
  601.9 909.5 %all-reduce.5.cloned.1.call-start = ((), (), s32[]{:S(2)}) async-start(), calls=%async_computation.1 | async-start | bytes 12582912 | tf_op jit(solution)/shard_map/psum | solution.py:63
  846.6 6.4 copy-start
  853.0 66.8 %collective-permute-start.4 = (f32[15,96,1024]{2,1,0:T(8,128)}, f32[15,96,1024]{2,1,0:T(8,128)}, u32[]{:S(2)}, u32[]{:S(2)}) collective-permute-start(f32[15,96,1024]{2,1,0:T(8,128)} %get-tuple-element.7), channel_id=1, source_target_pairs={{0,1},{1,2},{2,3},{3,4},{4,5},{5,6},{6,7},{7,8},{8,9},{9,10},{10,1... | collective-permute-start | bytes 17694728 | tf_op jit(solution)/shard_map/ppermute | solution.py:18
  855.8 129.8 %collective-permute-start.5 = (f32[15,96,1024]{2,1,0:T(8,128)}, f32[15,96,1024]{2,1,0:T(8,128)}, u32[]{:S(2)}, u32[]{:S(2)}) collective-permute-start(f32[15,96,1024]{2,1,0:T(8,128)} %get-tuple-element.8), channel_id=1, source_target_pairs={{1,0},{2,1},{3,2},{4,3},{5,4},{6,5},{7,6},{8,7},{9,8},{10,9},{11,1... | collective-permute-start | bytes 17694728 | tf_op jit(solution)/shard_map/ppermute | solution.py:19
  1172.0 128.4 %collective-permute-start.6 = (f32[15,96,1024]{2,1,0:T(8,128)}, f32[15,96,1024]{2,1,0:T(8,128)}, u32[]{:S(2)}, u32[]{:S(2)}) collective-permute-start(f32[15,96,1024]{2,1,0:T(8,128)} %get-tuple-element.5), channel_id=1, source_target_pairs={{1,0},{2,1},{3,2},{4,3},{5,4},{6,5},{7,6},{8,7},{9,8},{10,9},{11,1... | collective-permute-start | bytes 17694728 | tf_op jit(solution)/shard_map/ppermute | solution.py:19
  1174.2 126.3 %collective-permute-start.7 = (f32[15,96,1024]{2,1,0:T(8,128)}, f32[15,96,1024]{2,1,0:T(8,128)}, u32[]{:S(2)}, u32[]{:S(2)}) collective-permute-start(f32[15,96,1024]{2,1,0:T(8,128)} %get-tuple-element.6), channel_id=1, source_target_pairs={{0,1},{1,2},{2,3},{3,4},{4,5},{5,6},{6,7},{7,8},{8,9},{9,10},{10,1... | collective-permute-start | bytes 17694728 | tf_op jit(solution)/shard_map/ppermute | solution.py:18
Sparse Core Ops, SparseCore 0:
  602.0 152.2 all-reduce.2
  1364.6 146.7 all-reduce.4
where the time goes:
time: 1540 us; the launch traced here: 1530 us
  waiting for transfers between devices  795 us (52%)
  matrix products  526 us (34%)
  other arithmetic  140 us (9%)
  local copies, waits for them, and re-layouts  28.3 us (2%)
  starting transfers between devices  25.4 us (2%)
    dot_general x4, matrix products, xy_pass(): passed = jnp.dot(volume, mat_x, precision=lax.Precision.HIGHEST)  419 us
    ppermute x4, waiting for transfers between devices, padded_2(): after = lax.ppermute(initial, axis, down)  375 us
    psum x2, waiting for transfers between devices, per_device(): logsum = lax.psum(logs, 'view')  299 us
    log x2, other arithmetic, per_device(): logs = jnp.log(back)  128 us
    ppermute x4, waiting for transfers between devices, padded_2(): before = lax.ppermute(last, axis, up)  121 us
    dot_general x4, matrix products, xy_pass(): jnp.einsum('zyx,yw->zwx', passed, mat_y, precision=lax.Precision.HIGHEST)  107 us
  transfers between devices with their start and end apart: 10, of which 8 were waited for; matrix products, arithmetic and copies ran while one was open for 0% of the time, Pallas kernels for 0%

commit v1 on v0

--- a/solution.py
+++ b/solution.py
@@ -60,7 +60,7 @@
         ratio = data_slab / blurred
         back = z_pass(xy_pass(ratio, mat_x.T, mat_y.T), tap_norm[2], True)
         logs = jnp.log(back)
-        logsum = lax.psum(logs, "view")
+        logsum = jnp.sum(lax.all_gather(logs, "view"), axis=0)
         estimate = estimate * jnp.exp(logsum / views_count)
     return estimate
 

time: 1540 us -> 2270 us (1.47)
  waiting for transfers between devices: 795 us -> 1490 us
  other arithmetic: 140 us -> 180 us
    all_gather x0 -> x2, waiting for transfers between devices: none -> 996 us  [per_device(): logsum = jnp.sum(lax.all_gather(logs, 'view'), axis=0)]
    psum x2 -> x0, waiting for transfers between devices: 299 us -> none  [per_device(): logsum = lax.psum(logs, 'view')]
    reduce_sum x0 -> x2, other arithmetic: none -> 42.2 us  [per_device(): logsum = jnp.sum(lax.all_gather(logs, 'view'), axis=0)]
where the time goes in v1:
time: 2270 us; the launch traced here: 2260 us
  waiting for transfers between devices  1490 us (66%)
  matrix products  520 us (23%)
  other arithmetic  180 us (8%)
  local copies, waits for them, and re-layouts  27.9 us (1%)
  starting transfers between devices  25.4 us (1%)
    all_gather x2, waiting for transfers between devices, per_device(): logsum = jnp.sum(lax.all_gather(logs, 'view'), axis=0)  996 us
    dot_general x4, matrix products, xy_pass(): passed = jnp.dot(volume, mat_x, precision=lax.Precision.HIGHEST)  413 us
    ppermute x4, waiting for transfers between devices, padded_2(): after = lax.ppermute(initial, axis, down)  375 us
    log x2, other arithmetic, per_device(): logs = jnp.log(back)  126 us
    ppermute x4, waiting for transfers between devices, padded_2(): before = lax.ppermute(last, axis, up)  121 us
    dot_general x4, matrix products, xy_pass(): jnp.einsum('zyx,yw->zwx', passed, mat_y, precision=lax.Precision.HIGHEST)  108 us
  transfers between devices with their start and end apart: 10, of which 8 were waited for; matrix products, arithmetic and copies ran while one was open for 0% of the time, Pallas kernels for 0%

profile of v1, /device:TPU:1, one launch (start us, length us, event | category | flops | bytes accessed | tf_op | source)
XLA Modules:
  0.0 2259.3 jit_solution(6561220825755036773)
XLA Ops:
  11.0 45.1 %fusion.432 = f32[1024,16,96]{0,2,1:T(8,128)S(1)} fusion(f32[16,96,1024]{2,1,0:T(8,128)} %param.4, f32[]{:T(128)} %bitcast.65, f32[]{:T(128)} %bitcast.64, f32[]{:T(128)} %bitcast.63, f32[]{:T(128)} %bitcast.62, f32[]{:T(128)} %bitcast.61, f32[]{:T(128)} %bitcast.60, f32[]{:T(128)} %bitcast.59, f32[]{:T(128)} %bitcast.58, f32[]{:T(128)} %bitcast.57, ...), kind=kOutput, calls=%fused_computation.606 | convolution fusion | flops 19425918976 | bytes 12583036 | tf_op jit(solution)/shard_map/dot_general | solution.py:48
  56.1 26.3 %fusion.527 = f32[16,96,1024]{2,1,0:T(8,128)S(1)} fusion(f32[1024,16,96]{0,2,1:T(8,128)S(1)} %fusion.432, f32[]{:T(128)} %bitcast.31, f32[]{:T(128)} %bitcast.30, f32[]{:T(128)} %bitcast.29, f32[]{:T(128)} %bitcast.28, f32[]{:T(128)} %bitcast.27, f32[]{:T(128)} %bitcast.26, f32[]{:T(128)} %bitcast.25, f32[]{:T(128)} %bitcast.24, f32[]{:T(128)} %bitcast.23, ...), kind=kOutput, calls=%fused_computation.703 | convolution fusion | flops 1812805632 | bytes 12583036 | tf_op jit(solution)/shard_map/zyx,yw->zwx/dot_general | solution.py:49
  82.4 6.4 fusion.827
  96.6 60.8 %collective-permute-done = f32[15,96,1024]{2,1,0:T(8,128)} collective-permute-done((f32[15,96,1024]{2,1,0:T(8,128)}, f32[15,96,1024]{2,1,0:T(8,128)}, u32[]{:S(2)}, u32[]{:S(2)}) %collective-permute-start) | collective-permute-done | bytes 5898272 | tf_op jit(solution)/shard_map/ppermute | solution.py:18
  157.4 65.2 %collective-permute-done.1 = f32[15,96,1024]{2,1,0:T(8,128)} collective-permute-done((f32[15,96,1024]{2,1,0:T(8,128)}, f32[15,96,1024]{2,1,0:T(8,128)}, u32[]{:S(2)}, u32[]{:S(2)}) %collective-permute-start.1) | collective-permute-done | bytes 5898272 | tf_op jit(solution)/shard_map/ppermute | solution.py:19
  222.5 151.4 %fusion.295 = f32[16,96,1024]{2,1,0:T(8,128)} fusion(f32[16,96,1024]{2,1,0:T(8,128)} %copy-done.1, f32[15,96,1024]{2,1,0:T(8,128)} %collective-permute-done.1, f32[15,96,1024]{2,1,0:T(8,128)} %collective-permute-done, f32[1,16,96,1024]{3,2,1,0:T(8,128)} %param.3, f32[]{:T(128)} %bitcast.98, f32[]{:T(128)} %bitcast.97, f32[]{:T(128)} %bitcast.96, ...), kind=kOutput, calls=%fused_computation.491 | convolution fusion | flops 19570622464 | bytes 30671096 | tf_op jit(solution)/shard_map/dot_general | solution.py:48
  374.0 27.7 %convolution_bitcast_fusion.2 = f32[16,96,1024]{2,1,0:T(8,128)S(1)} fusion(f32[16,96,1024]{2,1,0:T(8,128)} %fusion.295, f32[]{:T(128)} %bitcast.31, f32[]{:T(128)} %bitcast.30, f32[]{:T(128)} %bitcast.29, f32[]{:T(128)} %bitcast.28, f32[]{:T(128)} %bitcast.27, f32[]{:T(128)} %bitcast.26, f32[]{:T(128)} %bitcast.25, f32[]{:T(128)} %bitcast.24, ...), kind=kOutput, calls=%fused_computation.706 | convolution fusion | flops 1812805632 | bytes 12583036 | tf_op jit(solution)/shard_map/zyx,yw->zwx/dot_general | solution.py:49
  401.6 6.0 fusion.826
  413.4 121.8 %collective-permute-done.2 = f32[15,96,1024]{2,1,0:T(8,128)} collective-permute-done((f32[15,96,1024]{2,1,0:T(8,128)}, f32[15,96,1024]{2,1,0:T(8,128)}, u32[]{:S(2)}, u32[]{:S(2)}) %collective-permute-start.2) | collective-permute-done | bytes 5898272 | tf_op jit(solution)/shard_map/ppermute | solution.py:19
  535.1 63.1 %fusion.207 = f32[16,96,1024]{2,1,0:T(8,128)} fusion(f32[16,96,1024]{2,1,0:T(8,128)S(1)} %convolution_bitcast_fusion.2, f32[15,96,1024]{2,1,0:T(8,128)} %collective-permute-done.3, f32[15,96,1024]{2,1,0:T(8,128)} %collective-permute-done.2, f32[]{:T(128)} %bitcast.98, f32[]{:T(128)} %bitcast.97, f32[]{:T(128)} %bitcast.96, f32[]{:T(128)} %bitcast.95, ...), kind=kLoop, calls=%fused_computation.403 | loop fusion | flops 143130624 | bytes 24379516 | tf_op jit(solution)/shard_map/log | solution.py:62
  598.3 500.2 %all-gather.5.cloned.1.call-done = f32[128,96,1024]{2,1,0:T(8,128)} async-done(((f32[16,96,1024]{2,1,0:T(8,128)}), f32[128,96,1024]{2,1,0:T(8,128)}) %all-gather.5.cloned.1.call-update) | async-done | bytes 50331664 | tf_op jit(solution)/shard_map/all_gather | solution.py:63
  1098.6 21.2 reduce_sum.28
  1119.7 65.8 %fusion.429 = f32[16,96,1024]{2,1,0:T(8,128)S(1)} fusion(f32[]{:T(128)} %bitcast.65, f32[]{:T(128)} %bitcast.64, f32[]{:T(128)} %bitcast.63, f32[]{:T(128)} %bitcast.62, f32[]{:T(128)} %bitcast.61, f32[]{:T(128)} %bitcast.60, f32[]{:T(128)} %bitcast.59, f32[]{:T(128)} %bitcast.58, f32[]{:T(128)} %bitcast.57, f32[]{:T(128)} %bitcast.56, f32[]{:T(128)} %bitcast.55, ...), kind=kOutput, calls=%fused_computation.603 | convolution fusion | flops 19429064704 | bytes 18874492 | tf_op jit(solution)/shard_map/dot_general | solution.py:48
  1185.6 25.9 %convolution_bitcast_fusion.1 = f32[16,96,1024]{2,1,0:T(8,128)S(1)} fusion(f32[16,96,1024]{2,1,0:T(8,128)S(1)} %fusion.429, f32[]{:T(128)} %bitcast.31, f32[]{:T(128)} %bitcast.30, f32[]{:T(128)} %bitcast.29, f32[]{:T(128)} %bitcast.28, f32[]{:T(128)} %bitcast.27, f32[]{:T(128)} %bitcast.26, f32[]{:T(128)} %bitcast.25, f32[]{:T(128)} %bitcast.24, ...), kind=kOutput, calls=%fused_computation.705 | convolution fusion | flops 1812805632 | bytes 12583036 | tf_op jit(solution)/shard_map/zyx,yw->zwx/dot_general | solution.py:49
  1211.5 6.2 fusion.825
  1224.4 60.4 %collective-permute-done.4 = f32[15,96,1024]{2,1,0:T(8,128)} collective-permute-done((f32[15,96,1024]{2,1,0:T(8,128)}, f32[15,96,1024]{2,1,0:T(8,128)}, u32[]{:S(2)}, u32[]{:S(2)}) %collective-permute-start.4) | collective-permute-done | bytes 5898272 | tf_op jit(solution)/shard_map/ppermute | solution.py:18
  1284.8 65.8 %collective-permute-done.5 = f32[15,96,1024]{2,1,0:T(8,128)} collective-permute-done((f32[15,96,1024]{2,1,0:T(8,128)}, f32[15,96,1024]{2,1,0:T(8,128)}, u32[]{:S(2)}, u32[]{:S(2)}) %collective-permute-start.5) | collective-permute-done | bytes 5898272 | tf_op jit(solution)/shard_map/ppermute | solution.py:19
  1350.6 150.2 %fusion.92 = f32[16,96,1024]{2,1,0:T(8,128)} fusion(f32[16,96,1024]{2,1,0:T(8,128)} %copy-done, f32[15,96,1024]{2,1,0:T(8,128)} %collective-permute-done.5, f32[15,96,1024]{2,1,0:T(8,128)} %collective-permute-done.4, f32[1,16,96,1024]{3,2,1,0:T(8,128)} %param.3, f32[]{:T(128)} %bitcast.98, f32[]{:T(128)} %bitcast.97, f32[]{:T(128)} %bitcast.96, ...), kind=kOutput, calls=%fused_computation.316 | convolution fusion | flops 19570622464 | bytes 30671096 | tf_op jit(solution)/shard_map/dot_general | solution.py:48
  1500.8 27.7 %convolution_bitcast_fusion = f32[16,96,1024]{2,1,0:T(8,128)S(1)} fusion(f32[16,96,1024]{2,1,0:T(8,128)} %fusion.92, f32[]{:T(128)} %bitcast.31, f32[]{:T(128)} %bitcast.30, f32[]{:T(128)} %bitcast.29, f32[]{:T(128)} %bitcast.28, f32[]{:T(128)} %bitcast.27, f32[]{:T(128)} %bitcast.26, f32[]{:T(128)} %bitcast.25, f32[]{:T(128)} %bitcast.24, f32[]{:T(128)} %bitcast.23, ...), kind=kOutput, calls=%fused_computation.704 | convolution fusion | flops 1812805632 | bytes 12583036 | tf_op jit(solution)/shard_map/zyx,yw->zwx/dot_general | solution.py:49
  1540.2 122.6 %collective-permute-done.6 = f32[15,96,1024]{2,1,0:T(8,128)} collective-permute-done((f32[15,96,1024]{2,1,0:T(8,128)}, f32[15,96,1024]{2,1,0:T(8,128)}, u32[]{:S(2)}, u32[]{:S(2)}) %collective-permute-start.6) | collective-permute-done | bytes 5898272 | tf_op jit(solution)/shard_map/ppermute | solution.py:19
  1662.8 62.9 %fusion.4 = f32[16,96,1024]{2,1,0:T(8,128)} fusion(f32[16,96,1024]{2,1,0:T(8,128)S(1)} %convolution_bitcast_fusion, f32[15,96,1024]{2,1,0:T(8,128)} %collective-permute-done.7, f32[15,96,1024]{2,1,0:T(8,128)} %collective-permute-done.6, f32[]{:T(128)} %bitcast.98, f32[]{:T(128)} %bitcast.97, f32[]{:T(128)} %bitcast.96, f32[]{:T(128)} %bitcast.95, ...), kind=kLoop, calls=%fused_computation.228 | loop fusion | flops 143130624 | bytes 24379516 | tf_op jit(solution)/shard_map/log | solution.py:62
  1725.7 495.3 %all-gather.7.cloned.1.call-done = f32[128,96,1024]{2,1,0:T(8,128)} async-done(((f32[16,96,1024]{2,1,0:T(8,128)}), f32[128,96,1024]{2,1,0:T(8,128)}) %all-gather.7.cloned.1.call-update) | async-done | bytes 50331664 | tf_op jit(solution)/shard_map/all_gather | solution.py:63
  2221.0 21.1 reduce_sum.29
  2242.1 9.9 exponential_multiply_fusion
  (26 shorter events, 36.5 us)
Async XLA Ops:
  6.5 1092.0 %all-gather.5.cloned.1.call-start = ((), (), s32[]{:S(2)}) async-start(), calls=%async_computation | async-start | bytes 56623104 | tf_op jit(solution)/shard_map/all_gather | solution.py:63
  82.4 6.4 copy-start.1
  88.8 68.6 %collective-permute-start = (f32[15,96,1024]{2,1,0:T(8,128)}, f32[15,96,1024]{2,1,0:T(8,128)}, u32[]{:S(2)}, u32[]{:S(2)}) collective-permute-start(f32[15,96,1024]{2,1,0:T(8,128)} %get-tuple-element.11), channel_id=1, source_target_pairs={{0,1},{1,2},{2,3},{3,4},{4,5},{5,6},{6,7},{7,8},{8,9},{9,10},{10,1... | collective-permute-start | bytes 17694728 | tf_op jit(solution)/shard_map/ppermute | solution.py:18
  93.4 129.2 %collective-permute-start.1 = (f32[15,96,1024]{2,1,0:T(8,128)}, f32[15,96,1024]{2,1,0:T(8,128)}, u32[]{:S(2)}, u32[]{:S(2)}) collective-permute-start(f32[15,96,1024]{2,1,0:T(8,128)} %get-tuple-element.12), channel_id=1, source_target_pairs={{1,0},{2,1},{3,2},{4,3},{5,4},{6,5},{7,6},{8,7},{9,8},{10,9},{11,1... | collective-permute-start | bytes 17694728 | tf_op jit(solution)/shard_map/ppermute | solution.py:19
  407.6 127.5 %collective-permute-start.2 = (f32[15,96,1024]{2,1,0:T(8,128)}, f32[15,96,1024]{2,1,0:T(8,128)}, u32[]{:S(2)}, u32[]{:S(2)}) collective-permute-start(f32[15,96,1024]{2,1,0:T(8,128)} %get-tuple-element.9), channel_id=1, source_target_pairs={{1,0},{2,1},{3,2},{4,3},{5,4},{6,5},{7,6},{8,7},{9,8},{10,9},{11,1... | collective-permute-start | bytes 17694728 | tf_op jit(solution)/shard_map/ppermute | solution.py:19
  409.7 125.4 %collective-permute-start.3 = (f32[15,96,1024]{2,1,0:T(8,128)}, f32[15,96,1024]{2,1,0:T(8,128)}, u32[]{:S(2)}, u32[]{:S(2)}) collective-permute-start(f32[15,96,1024]{2,1,0:T(8,128)} %get-tuple-element.10), channel_id=1, source_target_pairs={{0,1},{1,2},{2,3},{3,4},{4,5},{5,6},{6,7},{7,8},{8,9},{9,10},{10,1... | collective-permute-start | bytes 17694728 | tf_op jit(solution)/shard_map/ppermute | solution.py:18
  598.3 1622.8 %all-gather.7.cloned.1.call-start = ((), (), s32[]{:S(2)}) async-start(), calls=%async_computation.1 | async-start | bytes 56623104 | tf_op jit(solution)/shard_map/all_gather | solution.py:63
  1211.5 6.2 copy-start
  1217.6 67.2 %collective-permute-start.4 = (f32[15,96,1024]{2,1,0:T(8,128)}, f32[15,96,1024]{2,1,0:T(8,128)}, u32[]{:S(2)}, u32[]{:S(2)}) collective-permute-start(f32[15,96,1024]{2,1,0:T(8,128)} %get-tuple-element.7), channel_id=1, source_target_pairs={{0,1},{1,2},{2,3},{3,4},{4,5},{5,6},{6,7},{7,8},{8,9},{9,10},{10,1... | collective-permute-start | bytes 17694728 | tf_op jit(solution)/shard_map/ppermute | solution.py:18
  1220.8 129.8 %collective-permute-start.5 = (f32[15,96,1024]{2,1,0:T(8,128)}, f32[15,96,1024]{2,1,0:T(8,128)}, u32[]{:S(2)}, u32[]{:S(2)}) collective-permute-start(f32[15,96,1024]{2,1,0:T(8,128)} %get-tuple-element.8), channel_id=1, source_target_pairs={{1,0},{2,1},{3,2},{4,3},{5,4},{6,5},{7,6},{8,7},{9,8},{10,9},{11,1... | collective-permute-start | bytes 17694728 | tf_op jit(solution)/shard_map/ppermute | solution.py:19
  1534.3 128.4 %collective-permute-start.6 = (f32[15,96,1024]{2,1,0:T(8,128)}, f32[15,96,1024]{2,1,0:T(8,128)}, u32[]{:S(2)}, u32[]{:S(2)}) collective-permute-start(f32[15,96,1024]{2,1,0:T(8,128)} %get-tuple-element.5), channel_id=1, source_target_pairs={{1,0},{2,1},{3,2},{4,3},{5,4},{6,5},{7,6},{8,7},{9,8},{10,9},{11,1... | collective-permute-start | bytes 17694728 | tf_op jit(solution)/shard_map/ppermute | solution.py:19
  1536.5 126.3 %collective-permute-start.7 = (f32[15,96,1024]{2,1,0:T(8,128)}, f32[15,96,1024]{2,1,0:T(8,128)}, u32[]{:S(2)}, u32[]{:S(2)}) collective-permute-start(f32[15,96,1024]{2,1,0:T(8,128)} %get-tuple-element.6), channel_id=1, source_target_pairs={{0,1},{1,2},{2,3},{3,4},{4,5},{5,6},{6,7},{7,8},{8,9},{9,10},{10,1... | collective-permute-start | bytes 17694728 | tf_op jit(solution)/shard_map/ppermute | solution.py:18
Sparse Core Ops, SparseCore 0:
  598.4 500.1 all-gather.4
  1725.9 495.1 all-gather.6
